TPU v7x, 512 devices: a whole 4x8x8 slice. The times are simulated.
512 devices in a mesh: xy: 32 (over z, x_lo, core), gz: 16 (over y, x_hi).
Axes of the slice: x: 4 (x_hi: 2, x_lo: 2; x = x_hi * 2 + x_lo), y: 8, z: 8, core: 2. Of those that a mesh axis runs over, the one named last changes fastest.
Arguments:
- volume: bfloat16 [64, 128, 128, 128], P('xy', None, 'gz'), may hold values from -6 to 6
- conv_first: bfloat16 [3, 3, 128, 128], replicated, may hold values from -0.1875 to 0.1875
- conv_second: bfloat16 [3, 3, 128, 128], replicated, may hold values from -0.1875 to 0.1875
- w_qkv: bfloat16 [128, 384], replicated
- w_out: bfloat16 [128, 128], replicated, may hold values from -0.5 to 0.5
Outputs:
- refined: bfloat16 [64, 128, 128, 128], P('xy', None, 'gz')
All inputs are finite; a program needn't handle non-finite values.
Results may differ from a plain program's by a relative error of at most 0.0085.
Values may be sent and summed in bfloat16 or wider, within the bound.
No kernel may reach another device: no remote copies, remote signals or barrier semaphores. Data moves between devices by JAX's collectives and lax.ppermute only.
A program may use at most 64 MiB of HBM per device.

v0:
```python
import jax
import jax.numpy as jnp
from jax import lax
from jax.sharding import PartitionSpec as P

HEADS = 4


def padded_2(block, sides, width):
    for axis, dim in sides:
        count = lax.axis_size(axis)
        forward = [(i, i + 1) for i in range(count - 1)]
        backward = [(target, source) for source, target in forward]
        low = lax.ppermute(
            lax.slice_in_dim(block, block.shape[dim] - width, None, axis=dim), axis, forward
        )
        high = lax.ppermute(lax.slice_in_dim(block, 0, width, axis=dim), axis, backward)
        block = jnp.concatenate([low, block, high], axis=dim)
    return block


def conv_local(padded, weight, count):
    cols = padded.shape[1]
    wider = jnp.pad(padded, ((0, 0), (1, 1), (0, 0), (0, 0)))
    total = jnp.zeros((count,) + padded.shape[1:], jnp.float32)
    for shift_r in range(3):
        for shift_c in range(3):
            total = total + jnp.dot(
                wider[shift_r : shift_r + count, shift_c : shift_c + cols],
                weight[shift_r, shift_c],
                preferred_element_type=jnp.float32,
            )
    return total


def project(row, w_qkv):
    values = row.astype(jnp.float32)
    normed = values / jnp.sqrt(jnp.mean(values * values, axis=-1, keepdims=True) + 1e-06)
    return jnp.dot(normed, w_qkv.astype(jnp.float32), preferred_element_type=jnp.float32).astype(
        jnp.bfloat16
    )


def attend(qkv, w_out):
    cols, depth, triple = qkv.shape
    width = triple // 3
    split = qkv.reshape(cols, depth, 3, HEADS, width // HEADS)
    scores = jnp.einsum(
        "cqhd,ckhd->chqk", split[:, :, 0], split[:, :, 1], preferred_element_type=jnp.float32
    )
    scores = scores / jnp.sqrt(jnp.float32(width // HEADS))
    probs = jax.nn.softmax(scores, axis=-1).astype(jnp.bfloat16)
    context = jnp.einsum(
        "chqk,ckhd->cqhd", probs, split[:, :, 2], preferred_element_type=jnp.float32
    ).astype(jnp.bfloat16)
    return jnp.dot(
        context.reshape(cols, depth, width), w_out, preferred_element_type=jnp.float32
    ).astype(jnp.bfloat16)


def on_device(volume, conv_first, conv_second, w_qkv, w_out):
    count = volume.shape[0]
    padded = padded_2(volume, (("xy", 0),), 2)
    hidden = jax.nn.silu(conv_local(padded, conv_first, count + 2)).astype(jnp.bfloat16)
    position = lax.axis_index("xy") * count - 1 + jnp.arange(count + 2, dtype=jnp.int32)
    inside = (position >= 0) & (position < count * lax.axis_size("xy"))
    hidden = jnp.where(inside[:, None, None, None], hidden, jnp.zeros_like(hidden))
    second = conv_local(hidden, conv_second, count)
    mixed = (volume.astype(jnp.float32) + second).astype(jnp.bfloat16)
    attended = lax.map(
        lambda row: attend(project(row, w_qkv), w_out),
        lax.all_to_all(mixed, "gz", split_axis=1, concat_axis=2, tiled=True),
    )
    returned = lax.all_to_all(attended, "gz", split_axis=2, concat_axis=1, tiled=True)
    return (mixed.astype(jnp.float32) + returned.astype(jnp.float32)).astype(jnp.bfloat16)


def solution(mesh):
    placed = (P("xy", None, "gz", None), P(), P(), P(), P())
    return jax.shard_map(
        on_device, mesh=mesh, in_specs=placed, out_specs=P("xy", None, "gz", None), check_vma=False
    )
```

profile of v0, /device:TPU:194, one launch (start us, length us, event | category | flops | bytes accessed | tf_op | source)
XLA Modules:
  0.0 89.7 jit_solution(1465598355060137577)
XLA Ops:
  0.0 0.0 copy-start
  0.0 0.0 copy-start.2
  0.0 1.2 %copy.41 = bf16[2,128,8,128]{3,1,2,0:T(8,128)(2,1)S(1)} copy(bf16[2,128,8,128]{3,2,1,0:T(8,128)(2,1)} %param.7) | data formatting | bytes 1048576 | tf_op args[0]
  1.2 1.9 %collective-permute-start = (bf16[2,128,8,128]{3,1,2,0:T(8,128)(2,1)S(1)}, bf16[2,128,8,128]{3,1,2,0:T(8,128)(2,1)S(1)}, u32[]{:S(2)}, u32[]{:S(2)}) collective-permute-start(bf16[2,128,8,128]{3,1,2,0:T(8,128)(2,1)S(1)} %copy.41), channel_id=1, source_target_pairs={{0,16},{16,32},{32,48},{48,64},{64,80},{80,96},{96,112},{112,128},... | collective-permute-start | bytes 1572872 | tf_op jit(solution)/shard_map/ppermute | solution.py:14
  3.1 3.6 %collective-permute-start.1 = (bf16[2,128,8,128]{3,1,2,0:T(8,128)(2,1)S(1)}, bf16[2,128,8,128]{3,1,2,0:T(8,128)(2,1)S(1)}, u32[]{:S(2)}, u32[]{:S(2)}) collective-permute-start(bf16[2,128,8,128]{3,1,2,0:T(8,128)(2,1)S(1)} %copy.41), channel_id=1, source_target_pairs={{16,0},{32,16},{48,32},{64,48},{80,64},{96,80},{112,96},{128,112},... | collective-permute-start | bytes 1572872 | tf_op jit(solution)/shard_map/ppermute | solution.py:17
  6.8 4.9 %collective-permute-done = bf16[2,128,8,128]{3,1,2,0:T(8,128)(2,1)S(1)} collective-permute-done((bf16[2,128,8,128]{3,1,2,0:T(8,128)(2,1)S(1)}, bf16[2,128,8,128]{3,1,2,0:T(8,128)(2,1)S(1)}, u32[]{:S(2)}, u32[]{:S(2)}) %collective-permute-start) | collective-permute-done | bytes 524320 | tf_op jit(solution)/shard_map/ppermute | solution.py:14
  11.8 0.0 copy-done
  11.8 0.1 constant_dynamic-update-slice_fusion.1
  11.9 4.4 %collective-permute-done.1 = bf16[2,128,8,128]{3,1,2,0:T(8,128)(2,1)S(1)} collective-permute-done((bf16[2,128,8,128]{3,1,2,0:T(8,128)(2,1)S(1)}, bf16[2,128,8,128]{3,1,2,0:T(8,128)(2,1)S(1)}, u32[]{:S(2)}, u32[]{:S(2)}) %collective-permute-start.1) | collective-permute-done | bytes 524320 | tf_op jit(solution)/shard_map/ppermute | solution.py:17
  16.3 0.1 constant_dynamic-update-slice_fusion
  16.4 0.0 copy-done.2
  16.4 0.4 fusion.36
  16.8 0.4 fusion.38
  17.3 0.4 fusion.40
  17.7 0.4 fusion.42
  18.1 0.4 fusion.44
  18.6 0.4 fusion.71
  19.0 0.4 fusion.20
  19.4 0.4 fusion.24
  19.8 0.0 copy-start.3
  19.9 1.4 %fusion.33 = bf16[4,128,8,128]{3,1,2,0:T(8,128)(2,1)S(1)} fusion(f32[4,128,8,128]{3,1,2,0:T(8,128)S(1)} %fusion.24, f32[4,128,8,128]{3,1,2,0:T(8,128)S(1)} %fusion.36, f32[4,128,8,128]{3,1,2,0:T(8,128)S(1)} %fusion.38, f32[4,128,8,128]{3,1,2,0:T(8,128)S(1)} %fusion.71, f32[4,128,8,128]{3,1,2,0:T(8,128)S(1)} %fusion.40, f32[4,128,8,128]{3,1,2,0:T(8,128)S(1)} %fusion.42, ...), kind=kOutput, calls=%fused_computation.49 | convolution fusion | flops 141557760 | bytes 19431936 | tf_op jit(solution)/shard_map/dot_general | solution.py:28
  21.2 0.0 copy-done.3
  21.2 0.3 fusion.52
  21.5 0.3 fusion.53
  21.8 0.3 fusion.54
  22.1 0.3 fusion.55
  22.4 0.3 fusion.56
  22.7 0.3 fusion.57
  23.0 0.3 fusion.18
  23.3 0.3 fusion.16
  23.6 0.3 fusion.19
  24.0 0.0 copy-start.1
  24.0 0.0 copy-start.4
  24.0 1.1 %copy.47 = bf16[2,128,8,128]{3,2,0,1:T(8,128)(2,1)} copy(bf16[2,128,8,128]{3,1,2,0:T(8,128)(2,1)S(1)} %fusion.19) | data formatting | bytes 1048576 | tf_op jit(solution)/shard_map/convert_element_type | solution.py:69
  25.1 9.1 %all-to-all-start = ((bf16[2,128,8,128]{3,2,0,1:T(8,128)(2,1)}), bf16[2,128,8,128]{3,2,0,1:T(8,128)(2,1)S(1)}, u32[]{:S(2)}, u32[]{:S(2)}) async-start(bf16[2,128,8,128]{3,2,0,1:T(8,128)(2,1)} %copy.47), calls=%async_computation | async-start | bytes 1048576 | tf_op jit(solution)/shard_map/all_to_all | solution.py:72
  34.2 18.3 %all-to-all-done = bf16[2,128,8,128]{3,2,0,1:T(8,128)(2,1)S(1)} async-done(((bf16[2,128,8,128]{3,2,0,1:T(8,128)(2,1)}), bf16[2,128,8,128]{3,2,0,1:T(8,128)(2,1)S(1)}, u32[]{:S(2)}, u32[]{:S(2)}) %all-to-all-start) | async-done | bytes 524320 | tf_op jit(solution)/shard_map/all_to_all | solution.py:72
  52.5 0.1 copy.84
  52.6 0.0 copy-done.1
  52.6 0.0 copy-done.4
  52.6 11.5 %while.10 = (s32[]{:T(128)}, bf16[2,8,128,128]{3,1,0,2:T(8,128)(2,1)S(1)}, bf16[2,8,128,128]{3,2,1,0:T(8,128)(2,1)S(1)}, bf16[128,384]{1,0:T(8,128)(2,1)S(1)}, bf16[128,128]{1,0:T(8,128)(2,1)S(1)}, /*index=5*/s32[]{:T(128)}) while((s32[]{:T(128)}, bf16[2,8,128,128]{3,1,0,2:T(8,128)(2,1)S(1)}, bf16[2,8,128,128]{3,2,1,0:T(8,128)(2,1)S(1)}, ...), condition=%wide.region_4.5_spmd, body=%wide.region_0.4_spmd.sunk | while | flops 205259904 | bytes 9355345 | solution.py:70
  52.7 0.2 fusion.125
  52.9 0.4 convolution_convert_fusion.5
  53.3 0.4 copy.88
  53.7 2.2 %fusion.126 = (f32[8,4,128]{2,1,0:T(4,128)S(1)}, f32[8,4,128,128]{2,3,1,0:T(8,128)}) fusion(bf16[8,128,3,4,32]{1,4,3,2,0:T(8,128)(2,1)S(1)} %bitcast.217), kind=kOutput, calls=%fused_computation.134.clone.1 | convolution fusion | flops 35127424 | bytes 2637824 | tf_op jit(solution)/shard_map/while/body/eval_jaxpr/sub | solution.py:52
  55.9 2.0 %convolution_convert_fusion.6 = bf16[8,4,32,128]{3,2,1,0:T(8,128)(2,1)S(1)} fusion(f32[8,4,128,128]{2,3,1,0:T(8,128)} %get-tuple-element.78, f32[8,4,128]{2,1,0:T(4,128)S(1)} %get-tuple-element.79, bf16[8,128,3,4,32]{1,4,3,2,0:T(8,128)(2,1)S(1)} %bitcast.218), kind=kOutput, calls=%fused_computation.7.clone.1 | convolution fusion | flops 34734080 | bytes 2637824 | tf_op jit(solution)/shard_map/while/body/eval_jaxpr/chqk,ckhd->cqhd/dot_general | solution.py:53
  57.9 0.3 fusion.127
  58.2 0.2 copy_dynamic-update-slice_fusion.2
  58.4 0.2 fusion.125
  58.7 0.4 convolution_convert_fusion.5
  59.1 0.4 copy.88
  59.5 2.2 %fusion.126 = (f32[8,4,128]{2,1,0:T(4,128)S(1)}, f32[8,4,128,128]{2,3,1,0:T(8,128)}) fusion(bf16[8,128,3,4,32]{1,4,3,2,0:T(8,128)(2,1)S(1)} %bitcast.217), kind=kOutput, calls=%fused_computation.134.clone.1 | convolution fusion | flops 35127424 | bytes 2637824 | tf_op jit(solution)/shard_map/while/body/eval_jaxpr/sub | solution.py:52
  61.7 2.0 %convolution_convert_fusion.6 = bf16[8,4,32,128]{3,2,1,0:T(8,128)(2,1)S(1)} fusion(f32[8,4,128,128]{2,3,1,0:T(8,128)} %get-tuple-element.78, f32[8,4,128]{2,1,0:T(4,128)S(1)} %get-tuple-element.79, bf16[8,128,3,4,32]{1,4,3,2,0:T(8,128)(2,1)S(1)} %bitcast.218), kind=kOutput, calls=%fused_computation.7.clone.1 | convolution fusion | flops 34734080 | bytes 2637824 | tf_op jit(solution)/shard_map/while/body/eval_jaxpr/chqk,ckhd->cqhd/dot_general | solution.py:53
  63.7 0.3 fusion.127
  64.0 0.2 copy_dynamic-update-slice_fusion.2
  64.2 24.2 %all_to_all.27 = bf16[2,8,128,128]{3,1,0,2:T(8,128)(2,1)S(1)} all-to-all(bf16[2,8,128,128]{3,1,0,2:T(8,128)(2,1)S(1)} %get-tuple-element.32), channel_id=1, replica_groups=mesh['xy'=32,'gz'=16] {'gz'}, dimensions={2} | all-to-all | bytes 1048576 | tf_op jit(solution)/shard_map/all_to_all | solution.py:74
  88.4 0.2 fusion.28
  88.5 1.1 %copy.51 = bf16[2,128,8,128]{3,2,1,0:T(8,128)(2,1)} copy(bf16[2,128,8,128]{3,1,2,0:T(8,128)(2,1)S(1)} %fusion.28) | data formatting | bytes 1048576 | tf_op jit(solution)/shard_map/convert_element_type | solution.py:75
  (5 shorter events, 0.1 us)
Async XLA Ops:
  0.0 11.8 %copy-start = (bf16[2,128,8,128]{3,2,1,0:T(8,128)(2,1)S(1)}, bf16[2,128,8,128]{3,2,1,0:T(8,128)(2,1)}, u32[]{:S(2)}) copy-start(bf16[2,128,8,128]{3,2,1,0:T(8,128)(2,1)} %param.7) | copy-start | bytes 1572868
  0.0 16.4 %copy-start.2 = (bf16[3,3,128,128]{3,2,1,0:T(8,128)(2,1)S(1)}, bf16[3,3,128,128]{3,2,1,0:T(8,128)(2,1)}, u32[]{:S(2)}) copy-start(bf16[3,3,128,128]{3,2,1,0:T(8,128)(2,1)} %param.8) | copy-start | bytes 884740
  1.2 10.5 %collective-permute-start = (bf16[2,128,8,128]{3,1,2,0:T(8,128)(2,1)S(1)}, bf16[2,128,8,128]{3,1,2,0:T(8,128)(2,1)S(1)}, u32[]{:S(2)}, u32[]{:S(2)}) collective-permute-start(bf16[2,128,8,128]{3,1,2,0:T(8,128)(2,1)S(1)} %copy.41), channel_id=1, source_target_pairs={{0,16},{16,32},{32,48},{48,64},{64,80},{80,96},{96,112},{112,128},... | collective-permute-start | bytes 1572872 | tf_op jit(solution)/shard_map/ppermute | solution.py:14
  3.1 13.1 %collective-permute-start.1 = (bf16[2,128,8,128]{3,1,2,0:T(8,128)(2,1)S(1)}, bf16[2,128,8,128]{3,1,2,0:T(8,128)(2,1)S(1)}, u32[]{:S(2)}, u32[]{:S(2)}) collective-permute-start(bf16[2,128,8,128]{3,1,2,0:T(8,128)(2,1)S(1)} %copy.41), channel_id=1, source_target_pairs={{16,0},{32,16},{48,32},{64,48},{80,64},{96,80},{112,96},{128,112},... | collective-permute-start | bytes 1572872 | tf_op jit(solution)/shard_map/ppermute | solution.py:17
  19.8 1.4 %copy-start.3 = (bf16[3,3,128,128]{3,2,1,0:T(8,128)(2,1)S(1)}, bf16[3,3,128,128]{3,2,1,0:T(8,128)(2,1)}, u32[]{:S(2)}) copy-start(bf16[3,3,128,128]{3,2,1,0:T(8,128)(2,1)} %param.9) | copy-start | bytes 884740
  24.0 28.7 %copy-start.1 = (bf16[128,128]{1,0:T(8,128)(2,1)S(1)}, bf16[128,128]{1,0:T(8,128)(2,1)}, u32[]{:S(2)}) copy-start(bf16[128,128]{1,0:T(8,128)(2,1)} %param.11) | copy-start | bytes 98308
  24.0 28.7 %copy-start.4 = (bf16[128,384]{1,0:T(8,128)(2,1)S(1)}, bf16[128,384]{1,0:T(8,128)(2,1)}, u32[]{:S(2)}) copy-start(bf16[128,384]{1,0:T(8,128)(2,1)} %param.10) | copy-start | bytes 294916
  25.1 27.4 %all-to-all-start = ((bf16[2,128,8,128]{3,2,0,1:T(8,128)(2,1)}), bf16[2,128,8,128]{3,2,0,1:T(8,128)(2,1)S(1)}, u32[]{:S(2)}, u32[]{:S(2)}) async-start(bf16[2,128,8,128]{3,2,0,1:T(8,128)(2,1)} %copy.47), calls=%async_computation | async-start | bytes 1048576 | tf_op jit(solution)/shard_map/all_to_all | solution.py:72
where the time goes:
time: 90 us; the launch traced here: 89.7 us
  waiting for transfers between devices  27.6 us (31%)
  blocking collectives  24.2 us (27%)
  matrix products  17.3 us (19%)
  starting transfers between devices  14.6 us (16%)
  local copies, waits for them, and re-layouts  5.06 us (6%)
    all_to_all x1, blocking collectives, on_device(): lax.all_to_all(attended, 'gz', split_axis=2, concat_axis=1, tiled=True)  24.2 us
    all_to_all x1, waiting for transfers between devices, on_device(): lax.all_to_all(mixed, 'gz', split_axis=1, concat_axis=2, tiled=True)  18.3 us
    all_to_all x1, starting transfers between devices, on_device(): lax.all_to_all(mixed, 'gz', split_axis=1, concat_axis=2, tiled=True)  9.05 us
    dot_general x18, matrix products, conv_local(): jnp.dot(wider[shift_r:shift_r + count, shift_c:shift_c + cols], weight[sh...  7.52 us
    ppermute x1, waiting for transfers between devices, padded_2(): lax.ppermute(lax.slice_in_dim(block, block.shape[dim] - width, None, axis...  4.9 us
    sub x2, matrix products, attend(): probs = jax.nn.softmax(scores, axis=-1).astype(jnp.bfloat16)  4.45 us
    ppermute x1, waiting for transfers between devices, padded_2(): lax.ppermute(lax.slice_in_dim(block, 0, width, axis=dim), axis, backward)  4.38 us
    dot_general x2, matrix products, attend(): jnp.einsum('chqk,ckhd->cqhd', probs, split[:, :, 2], preferred_element_ty...  3.93 us
  transfers between devices with their start and end apart: 3, of which 3 were waited for; matrix products, arithmetic and copies ran while one was open for 0% of the time, Pallas kernels for 0%

commit v1 on v0

v1 whole, which is shorter than its diff:
```python
import functools

import jax
import jax.numpy as jnp
from jax import lax
from jax.experimental import pallas as pl
from jax.experimental.pallas import tpu as pltpu
from jax.sharding import PartitionSpec as P

HEADS=4
F32=jnp.float32; BF=jnp.bfloat16

def blocks(weight):
    zero = jnp.zeros_like(weight[0])
    top = jnp.concatenate([jnp.concatenate([weight[0], zero], -1), jnp.concatenate([weight[1], weight[0]], -1)], -2)
    low = jnp.concatenate([jnp.concatenate([weight[2], weight[1]], -1), jnp.concatenate([zero, weight[2]], -1)], -2)
    ch2 = top.shape[-1]
    return jnp.concatenate([top.reshape(-1, ch2), low.reshape(-1, ch2)], 0)

def conv_kernel(tile, groups, edge, lo_ref, mid_ref, hi_ref, wa_ref, wb_ref, out_ref, xa, xs, ha, hs, wf1, wf2):
    cols, depth, ch = mid_ref.shape[1:]
    m = cols * depth
    for w_ref, wf in ((wa_ref, wf1), (wb_ref, wf2)):
        z = jnp.zeros((ch, ch), BF)
        for dc in range(3):
            b = dc * 2 * ch
            wf[b:b+ch, :ch] = w_ref[0, dc]
            wf[b:b+ch, ch:] = z
            wf[b+ch:b+2*ch, :ch] = w_ref[1, dc]
            wf[b+ch:b+2*ch, ch:] = w_ref[0, dc]
            b += 6 * ch
            wf[b:b+ch, :ch] = w_ref[2, dc]
            wf[b:b+ch, ch:] = w_ref[1, dc]
            wf[b+ch:b+2*ch, :ch] = z
            wf[b+ch:b+2*ch, ch:] = w_ref[2, dc]
    zrow = jnp.zeros((1, depth, ch), F32)
    srcs = [lo_ref.at[0], lo_ref.at[1], mid_ref.at[0], mid_ref.at[1], hi_ref.at[0], hi_ref.at[1]]
    for r, src in enumerate(srcs):
        v = src[...].astype(F32)
        xa[r] = v.reshape(m, ch).astype(BF)
        xs[r] = jnp.concatenate([zrow, v, zrow], 0).reshape(m + 2*depth, ch).astype(BF)
    steps = m // tile
    def gather(a, s, p, t):
        parts = []
        for dc in range(3):
            for r in (2*p, 2*p+1):
                if dc == 0: parts.append(s[r, pl.ds(t, tile)])
                elif dc == 1: parts.append(a[r, pl.ds(t, tile)])
                else: parts.append(s[r, pl.ds(t + 2*depth, tile)])
        return parts
    def conv(a, s, wf, p, t):
        lhs = jnp.concatenate(gather(a, s, p, t) + gather(a, s, p+1, t), axis=-1)
        return jnp.dot(lhs, wf[...], preferred_element_type=F32)
    for p in range(2):
        keep = edge[p]
        for k in range(steps):
            t = k * tile
            acc = conv(xa, xs, wf1, p, t)
            h = acc * (1.0 / (1.0 + jnp.exp(-acc)))
            for half in range(2):
                r = 2*p + half
                v = h[:, half*ch:(half+1)*ch]
                if r in (0, 3):
                    v = v * keep
                vb = v.astype(BF)
                ha[r, pl.ds(t, tile)] = vb
                hs[r, pl.ds(t + depth, tile)] = vb
    for r in range(4):
        hs[r, pl.ds(0, depth)] = jnp.zeros((depth, ch), BF)
        hs[r, pl.ds(m + depth, depth)] = jnp.zeros((depth, ch), BF)
    for k in range(steps):
        t = k * tile
        acc = conv(ha, hs, wf2, 0, t)
        c0 = t // depth
        nc = tile // depth
        for r in range(2):
            base = mid_ref[r, pl.ds(c0, nc)].astype(F32)
            res = base + acc[:, r*ch:(r+1)*ch].reshape(nc, depth, ch)
            res = res.astype(BF)
            g = cols // groups
            for j in range(nc // g):
                out_ref[c0 // g + j, r] = res[j*g:(j+1)*g]

def conv_block(lo, mid, hi, edge, conv_first, conv_second, groups=16, tile=256):
    rows, cols, depth, ch = mid.shape
    m = cols*depth
    vm = pl.BlockSpec(memory_space=pltpu.VMEM)
    return pl.pallas_call(
        functools.partial(lambda e, *r: conv_kernel(tile, groups, e, *r)),
        out_shape=jax.ShapeDtypeStruct((groups, rows, cols//groups, depth, ch), BF),
        in_specs=[pl.BlockSpec(memory_space=pltpu.SMEM)] + [vm]*5,
        out_specs=vm,
        scratch_shapes=[pltpu.VMEM((6, m, ch), BF), pltpu.VMEM((6, m+2*depth, ch), BF),
                        pltpu.VMEM((4, m, ch), BF), pltpu.VMEM((4, m+2*depth, ch), BF),
                        pltpu.VMEM((12*ch, 2*ch), BF), pltpu.VMEM((12*ch, 2*ch), BF)],
        compiler_params=pltpu.CompilerParams(vmem_limit_bytes=48<<20),
        name="conv_block",
    )(edge, lo, mid, hi, conv_first, conv_second)

def attend_kernel(x_ref, wq_ref, wo_ref, out_ref):
    parts, rows, cols, depth, ch = x_ref.shape
    sect = parts*depth
    hd = ch // HEADS
    scale = 1.4426950408889634 / (hd ** 0.5)
    lane = lax.broadcasted_iota(jnp.int32, (1, ch), 1) // hd
    masks = [(lane == h).astype(BF) for h in range(HEADS)]
    ones = jnp.concatenate([jnp.broadcast_to(mk, (sect, ch)) for mk in masks], 0)
    def cell(r, c):
        x = x_ref[:, r, c].astype(F32).reshape(sect, ch)
        n = (x * lax.rsqrt(jnp.mean(x*x, -1, keepdims=True) + 1e-6)).astype(BF)
        qkv = jnp.dot(n, wq_ref[...], preferred_element_type=F32).astype(BF)
        q, k, v = qkv[:, :ch], qkv[:, ch:2*ch], qkv[:, 2*ch:]
        ks = jnp.concatenate([k*mk for mk in masks], 0)
        vs = jnp.concatenate([v*mk for mk in masks], 0)
        s = lax.dot_general(q, ks, (((1,), (1,)), ((), ())), preferred_element_type=F32)
        ps = []
        for h in range(HEADS):
            sh = s[:, h*sect:(h+1)*sect]
            ps.append(jnp.exp2((sh - jnp.max(sh, -1, keepdims=True)) * scale).astype(BF))
        p = jnp.concatenate(ps, 1)
        pv = jnp.dot(p, jnp.concatenate([vs, ones], 1), preferred_element_type=F32)
        ctx = (pv[:, :ch] / pv[:, ch:]).astype(BF)
        o = jnp.dot(ctx, wo_ref[...], preferred_element_type=F32)
        out_ref[:, r, c] = o.reshape(parts, depth, ch).astype(BF)
    for r in range(rows):
        for c in range(cols):
            cell(r, c)

def attend_block(x, w_qkv, w_out):
    vm = pl.BlockSpec(memory_space=pltpu.VMEM)
    return pl.pallas_call(
        attend_kernel, out_shape=jax.ShapeDtypeStruct(x.shape, BF),
        in_specs=[vm]*3, out_specs=vm,
        compiler_params=pltpu.CompilerParams(vmem_limit_bytes=48<<20), name="attend_block",
    )(x, w_qkv, w_out)


def on_device(volume, conv_first, conv_second, w_qkv, w_out):
    count, groups = lax.axis_size("xy"), lax.axis_size("gz")
    forward = [(i, i + 1) for i in range(count - 1)]
    backward = [(target, source) for source, target in forward]
    low = lax.ppermute(volume, "xy", forward)
    high = lax.ppermute(volume, "xy", backward)
    place = lax.axis_index("xy")
    edge = jnp.stack([place > 0, place < count - 1]).astype(F32)
    mixed = conv_block(low, volume, high, edge, conv_first, conv_second, groups)
    arrived = lax.all_to_all(mixed, "gz", 0, 0, tiled=True)
    attended = attend_block(arrived, w_qkv, w_out)
    returned = lax.all_to_all(attended, "gz", 0, 0, tiled=True)
    total = (mixed.astype(F32) + returned.astype(F32)).astype(BF)
    return total.transpose(1, 0, 2, 3, 4).reshape(volume.shape)


def solution(mesh):
    placed = (P("xy", None, "gz", None), P(), P(), P(), P())
    return jax.shard_map(
        on_device, mesh=mesh, in_specs=placed, out_specs=P("xy", None, "gz", None), check_vma=False
    )
```

time: 90 us -> 83.7 us (0.930)
  the two profiles are of different devices: /device:TPU:194 before, /device:TPU:257 now
where the time goes in v1:
time: 83.7 us; the launch traced here: 83.3 us
  blocking collectives  48.4 us (58%)
  waiting for transfers between devices  12.7 us (15%)
  Pallas kernels  12.5 us (15%)
  starting transfers between devices  5.59 us (7%)
  local copies, waits for them, and re-layouts  3.81 us (5%)
    all_to_all x1, blocking collectives, on_device(): arrived = lax.all_to_all(mixed, 'gz', 0, 0, tiled=True)  26.4 us
    all_to_all x1, blocking collectives, on_device(): returned = lax.all_to_all(attended, 'gz', 0, 0, tiled=True)  21.9 us
    ppermute x1, waiting for transfers between devices, on_device(): low = lax.ppermute(volume, 'xy', forward)  10 us
    pallas_call x1, Pallas kernels, attend_block(): pl.pallas_call(attend_kernel, out_shape=jax.ShapeDtypeStruct(x.shape, BF)...  9.1 us
    ppermute x1, starting transfers between devices, on_device(): low = lax.ppermute(volume, 'xy', forward)  3.67 us
    pallas_call x1, Pallas kernels, conv_block(): pl.pallas_call(functools.partial(lambda e, *r: conv_kernel(tile, groups,...  3.44 us
    unnamed x10, local copies, waits for them, and re-layouts  2.98 us
    ppermute x1, waiting for transfers between devices, on_device(): high = lax.ppermute(volume, 'xy', backward)  2.7 us
  transfers between devices with their start and end apart: 2, of which 2 were waited for; matrix products, arithmetic and copies ran while one was open for 0% of the time, Pallas kernels for 0%

profile of v1, /device:TPU:257, one launch (start us, length us, event | category | flops | bytes accessed | tf_op | source)
XLA Modules:
  0.0 83.3 jit_solution(7894727813004388996)
XLA Ops:
  0.0 3.7 %collective-permute-start = (bf16[2,128,8,128]{3,2,1,0:T(8,128)(2,1)}, bf16[2,128,8,128]{3,2,1,0:T(8,128)(2,1)S(1)}, u32[]{:S(2)}, u32[]{:S(2)}) collective-permute-start(bf16[2,128,8,128]{3,2,1,0:T(8,128)(2,1)} %r_1_.1), channel_id=1, source_target_pairs={{0,16},{16,32},{32,48},{48,64},{64,80},{80,96},{96,112},{112,128},... | collective-permute-start | bytes 1572872 | tf_op jit(solution)/shard_map/ppermute | solution.py:142
  3.7 1.9 %collective-permute-start.1 = (bf16[2,128,8,128]{3,2,1,0:T(8,128)(2,1)}, bf16[2,128,8,128]{3,2,1,0:T(8,128)(2,1)S(1)}, u32[]{:S(2)}, u32[]{:S(2)}) collective-permute-start(bf16[2,128,8,128]{3,2,1,0:T(8,128)(2,1)} %r_1_.1), channel_id=1, source_target_pairs={{16,0},{32,16},{48,32},{64,48},{80,64},{96,80},{112,96},{128,112},... | collective-permute-start | bytes 1572872 | tf_op jit(solution)/shard_map/ppermute | solution.py:143
  5.6 0.1 add_convert_fusion.1.e
  5.7 10.0 %collective-permute-done.r_0_ = bf16[2,128,8,128]{3,2,1,0:T(8,128)(2,1)S(1)} collective-permute-done((bf16[2,128,8,128]{3,2,1,0:T(8,128)(2,1)}, bf16[2,128,8,128]{3,2,1,0:T(8,128)(2,1)S(1)}, u32[]{:S(2)}, u32[]{:S(2)}) %collective-permute-start) | collective-permute-done | bytes 524320 | tf_op jit(solution)/shard_map/ppermute | solution.py:142
  15.7 2.7 %collective-permute-done.1.r_2_ = bf16[2,128,8,128]{3,2,1,0:T(8,128)(2,1)S(1)} collective-permute-done((bf16[2,128,8,128]{3,2,1,0:T(8,128)(2,1)}, bf16[2,128,8,128]{3,2,1,0:T(8,128)(2,1)S(1)}, u32[]{:S(2)}, u32[]{:S(2)}) %collective-permute-start.1) | collective-permute-done | bytes 524320 | tf_op jit(solution)/shard_map/ppermute | solution.py:143
  18.4 0.0 copy-start
  18.4 1.0 %copy-done = bf16[2,128,8,128]{3,2,1,0:T(8,128)(2,1)S(1)} copy-done((bf16[2,128,8,128]{3,2,1,0:T(8,128)(2,1)S(1)}, bf16[2,128,8,128]{3,2,1,0:T(8,128)(2,1)}, u32[]{:S(2)}) %copy-start) | copy-done | bytes 524312
  19.5 0.0 copy-start.1
  19.5 1.0 %copy-done.1 = bf16[3,3,128,128]{3,2,1,0:T(8,128)(2,1)S(1)} copy-done((bf16[3,3,128,128]{3,2,1,0:T(8,128)(2,1)S(1)}, bf16[3,3,128,128]{3,2,1,0:T(8,128)(2,1)}, u32[]{:S(2)}) %copy-start.1) | copy-done | bytes 294936
  20.4 0.0 copy-start.2
  20.4 1.0 %copy-done.2 = bf16[3,3,128,128]{3,2,1,0:T(8,128)(2,1)S(1)} copy-done((bf16[3,3,128,128]{3,2,1,0:T(8,128)(2,1)S(1)}, bf16[3,3,128,128]{3,2,1,0:T(8,128)(2,1)}, u32[]{:S(2)}) %copy-start.2) | copy-done | bytes 294936
  21.4 3.4 %conv_block.1 = bf16[16,2,8,8,128]{4,3,2,1,0:T(8,128)(2,1)S(1)} custom-call(f32[2]{0:T(128)S(1)} %add_convert_fusion.1.e, bf16[2,128,8,128]{3,2,1,0:T(8,128)(2,1)S(1)} %collective-permute-done.r_0_, bf16[2,128,8,128]{3,2,1,0:T(8,128)(2,1)S(1)} %copy-done, bf16[2,128,8,128]{3,2,1,0:T(8,128)(2,1)S(1)} %collective-permute-done.1.r_2_, ...), custom_call_target="tpu_custom_call" | custom-call | tf_op jit(solution)/shard_map/conv_block/pallas_call | solution.py:88
  24.8 0.0 copy-start.3
  24.8 0.0 copy-start.4
  24.9 26.4 %all_to_all.10.x_ref = bf16[16,2,8,8,128]{4,3,2,1,0:T(8,128)(2,1)S(1)} all-to-all(bf16[16,2,8,8,128]{4,3,2,1,0:T(8,128)(2,1)S(1)} %conv_block.1), channel_id=1, replica_groups=mesh['xy'=32,'gz'=16] {'gz'}, dimensions={0} | all-to-all | bytes 1048576 | tf_op jit(solution)/shard_map/all_to_all | solution.py:147
  51.3 0.0 copy-done.3
  51.3 0.0 copy-done.4
  51.3 9.1 %attend_block.1 = bf16[16,2,8,8,128]{4,3,2,1,0:T(8,128)(2,1)S(1)} custom-call(bf16[16,2,8,8,128]{4,3,2,1,0:T(8,128)(2,1)S(1)} %all_to_all.10.x_ref, bf16[128,384]{1,0:T(8,128)(2,1)S(1)} %copy-done.3, bf16[128,128]{1,0:T(8,128)(2,1)S(1)} %copy-done.4), custom_call_target="tpu_custom_call" | custom-call | tf_op jit(solution)/shard_map/attend_block/pallas_call | solution.py:131
  60.4 21.9 %all_to_all.11 = bf16[16,2,8,8,128]{4,3,2,1,0:T(8,128)(2,1)S(1)} all-to-all(bf16[16,2,8,8,128]{4,3,2,1,0:T(8,128)(2,1)S(1)} %attend_block.1), channel_id=1, replica_groups=mesh['xy'=32,'gz'=16] {'gz'}, dimensions={0} | all-to-all | bytes 1048576 | tf_op jit(solution)/shard_map/all_to_all | solution.py:149
  82.3 0.2 fusion
  82.5 0.8 %copy.6 = bf16[2,16,8,8,128]{4,3,2,1,0:T(8,128)(2,1)} copy(bf16[2,16,8,8,128]{4,3,2,0,1:T(8,128)(2,1)S(1)} %fusion) | data formatting | bytes 1048576 | tf_op jit(solution)/shard_map/transpose | solution.py:151
Async XLA Ops:
  0.0 15.7 %collective-permute-start = (bf16[2,128,8,128]{3,2,1,0:T(8,128)(2,1)}, bf16[2,128,8,128]{3,2,1,0:T(8,128)(2,1)S(1)}, u32[]{:S(2)}, u32[]{:S(2)}) collective-permute-start(bf16[2,128,8,128]{3,2,1,0:T(8,128)(2,1)} %r_1_.1), channel_id=1, source_target_pairs={{0,16},{16,32},{32,48},{48,64},{64,80},{80,96},{96,112},{112,128},... | collective-permute-start | bytes 1572872 | tf_op jit(solution)/shard_map/ppermute | solution.py:142
  3.7 14.7 %collective-permute-start.1 = (bf16[2,128,8,128]{3,2,1,0:T(8,128)(2,1)}, bf16[2,128,8,128]{3,2,1,0:T(8,128)(2,1)S(1)}, u32[]{:S(2)}, u32[]{:S(2)}) collective-permute-start(bf16[2,128,8,128]{3,2,1,0:T(8,128)(2,1)} %r_1_.1), channel_id=1, source_target_pairs={{16,0},{32,16},{48,32},{64,48},{80,64},{96,80},{112,96},{128,112},... | collective-permute-start | bytes 1572872 | tf_op jit(solution)/shard_map/ppermute | solution.py:143
  18.4 1.0 %copy-start = (bf16[2,128,8,128]{3,2,1,0:T(8,128)(2,1)S(1)}, bf16[2,128,8,128]{3,2,1,0:T(8,128)(2,1)}, u32[]{:S(2)}) copy-start(bf16[2,128,8,128]{3,2,1,0:T(8,128)(2,1)} %r_1_.1) | copy-start | bytes 1572868
  19.5 1.0 %copy-start.1 = (bf16[3,3,128,128]{3,2,1,0:T(8,128)(2,1)S(1)}, bf16[3,3,128,128]{3,2,1,0:T(8,128)(2,1)}, u32[]{:S(2)}) copy-start(bf16[3,3,128,128]{3,2,1,0:T(8,128)(2,1)} %r_3_.1) | copy-start | bytes 884740
  20.4 1.0 %copy-start.2 = (bf16[3,3,128,128]{3,2,1,0:T(8,128)(2,1)S(1)}, bf16[3,3,128,128]{3,2,1,0:T(8,128)(2,1)}, u32[]{:S(2)}) copy-start(bf16[3,3,128,128]{3,2,1,0:T(8,128)(2,1)} %r_4_.1) | copy-start | bytes 884740
  24.8 26.4 %copy-start.3 = (bf16[128,384]{1,0:T(8,128)(2,1)S(1)}, bf16[128,384]{1,0:T(8,128)(2,1)}, u32[]{:S(2)}) copy-start(bf16[128,384]{1,0:T(8,128)(2,1)} %wq_ref.1) | copy-start | bytes 294916
  24.8 26.4 %copy-start.4 = (bf16[128,128]{1,0:T(8,128)(2,1)S(1)}, bf16[128,128]{1,0:T(8,128)(2,1)}, u32[]{:S(2)}) copy-start(bf16[128,128]{1,0:T(8,128)(2,1)} %wo_ref.1) | copy-start | bytes 98308

commit v2 on v0

v2 whole, which is shorter than its diff:
```python
import functools

import jax
import jax.numpy as jnp
from jax import lax
from jax.experimental import pallas as pl
from jax.experimental.pallas import tpu as pltpu
from jax.sharding import PartitionSpec as P

HEADS = 4
GROUP = 8
F32 = jnp.float32
BF = jnp.bfloat16


def vmem():
    return pl.BlockSpec(memory_space=pltpu.VMEM)


def cost(flops, moved):
    return pl.CostEstimate(flops=flops, bytes_accessed=moved, transcendentals=0)


def params():
    return pltpu.CompilerParams(vmem_limit_bytes=24 << 20)


def spread(value, flat, wide):
    cols, depth, ch = value.shape
    edge = jnp.zeros((1, depth, ch), F32)
    flat[...] = value.reshape(cols * depth, ch).astype(BF)
    wide[...] = jnp.concatenate([edge, value, edge], 0).reshape((cols + 2) * depth, ch).astype(BF)


def gather(flat, wide, r, t, tile, depth):
    parts = []
    for dc in range(3):
        for q in (r, r + 1):
            ref, at = (flat, t) if dc == 1 else (wide, t + dc * depth)
            parts.append(ref[q, pl.ds(at, tile)])
    return parts


def prepare_kernel(tile, vol, raw1, raw2, taps1, taps2, partial, again, flat, wide):
    again[...] = vol[...]
    cols, depth, ch = vol.shape[1:]
    m = cols * depth
    blank = jnp.zeros((ch, ch), BF)
    for raw, taps in ((raw1, taps1), (raw2, taps2)):
        for dc in range(3):
            quads = ((raw[0, dc], blank, raw[1, dc], raw[0, dc]), (raw[2, dc], raw[1, dc], blank, raw[2, dc]))
            for side in range(2):
                at = (side * 3 + dc) * 2 * ch
                for i in range(4):
                    taps[at + i // 2 * ch : at + (i // 2 + 1) * ch, i % 2 * ch : (i % 2 + 1) * ch] = quads[side][i]
    for r in range(2):
        spread(vol[r].astype(F32), flat.at[r], wide.at[r])
    k = 6 * ch
    for t in range(0, m, tile):
        lhs = jnp.concatenate(gather(flat, wide, 0, t, tile, depth), -1)
        for p in range(2):
            rhs = taps1[(1 - p) * k : (2 - p) * k]
            partial[p, pl.ds(t, tile)] = jnp.dot(lhs, rhs, preferred_element_type=F32)


def prepare(volume, first, second, tile=256):
    _, cols, depth, ch = volume.shape
    m = cols * depth
    return pl.pallas_call(
        functools.partial(prepare_kernel, tile),
        out_shape=[
            jax.ShapeDtypeStruct((12 * ch, 2 * ch), BF),
            jax.ShapeDtypeStruct((12 * ch, 2 * ch), BF),
            jax.ShapeDtypeStruct((2, m, 2 * ch), F32),
            jax.ShapeDtypeStruct(volume.shape, BF),
        ],
        in_specs=[vmem()] * 3,
        out_specs=[vmem()] * 4,
        scratch_shapes=[pltpu.VMEM((2, m, ch), BF), pltpu.VMEM((2, m + 2 * depth, ch), BF)],
        cost_estimate=cost(2 * 12 * ch * 2 * ch * m, 4 << 20),
        compiler_params=params(),
        name="prepare",
    )(volume, first, second)


def conv_kernel(tile, near, mid, far_a, far_b, taps1, taps2, partial, out_ref, xa, xs, ha, hs):
    cols, depth, ch = mid.shape[1:]
    m = cols * depth
    k = 6 * ch
    place = lax.axis_index("xy")
    odd = place % 2
    edge = [jnp.where(place == end, 0.0, 1.0).astype(F32) for end in (0, lax.axis_size("xy") - 1)]
    for r in range(2):
        at = 2 * (1 - odd) + r
        spread(near[r].astype(F32), xa.at[at], xs.at[at])
        at = 2 * odd + r
        spread(far_a[r].astype(F32) + far_b[r].astype(F32), xa.at[at], xs.at[at])
    blank = jnp.zeros((depth, ch), BF)
    for r in range(4):
        hs[r, pl.ds(0, depth)] = blank
        hs[r, pl.ds(m + depth, depth)] = blank
    for p in range(2):
        for t in range(0, m, tile):
            lhs = jnp.concatenate(gather(xa, xs, 2 * p, t, tile, depth), -1)
            acc = partial[p, pl.ds(t, tile)] + jnp.dot(lhs, taps1[p * k : (p + 1) * k], preferred_element_type=F32)
            h = acc * (1.0 / (1.0 + jnp.exp(-acc)))
            for half in range(2):
                r = 2 * p + half
                v = h[:, half * ch : (half + 1) * ch]
                if r in (0, 3):
                    v = v * edge[p]
                v = v.astype(BF)
                ha[r, pl.ds(t, tile)] = v
                hs[r, pl.ds(t + depth, tile)] = v
    per = cols // out_ref.shape[0]
    n = tile // depth
    for t in range(0, m, tile):
        lhs = gather(ha, hs, 0, t, tile, depth) + gather(ha, hs, 2, t, tile, depth)
        acc = jnp.dot(jnp.concatenate(lhs, -1), taps2[...], preferred_element_type=F32)
        for r in range(2):
            res = mid[r, pl.ds(t // depth, n)].astype(F32) + acc[:, r * ch : (r + 1) * ch].reshape(n, depth, ch)
            res = res.astype(BF)
            for j in range(n // per):
                out_ref[t // depth // per + j, r] = res[j * per : (j + 1) * per]


def conv_block(groups, prepared, near, mid, fars, tile=256):
    rows, cols, depth, ch = mid.shape
    m = cols * depth
    return pl.pallas_call(
        functools.partial(conv_kernel, tile),
        out_shape=jax.ShapeDtypeStruct((groups, rows, cols // groups, depth, ch), BF),
        in_specs=[vmem()] * 7,
        out_specs=vmem(),
        scratch_shapes=[
            pltpu.VMEM((4, m, ch), BF),
            pltpu.VMEM((4, m + 2 * depth, ch), BF),
            pltpu.VMEM((4, m, ch), BF),
            pltpu.VMEM((4, m + 2 * depth, ch), BF),
        ],
        cost_estimate=cost(4 * m * 12 * ch * 2 * ch, 4 << 20),
        compiler_params=params(),
        name="conv_block",
    )(near, mid, *fars, *prepared)


def attend_kernel(x_ref, wq_ref, wo_ref, out_ref):
    parts, rows, cols, depth, ch = x_ref.shape
    sect = parts * depth
    hd = ch // HEADS
    scale = 1.4426950408889634 / (hd**0.5)
    lane = lax.broadcasted_iota(jnp.int32, (1, ch), 1) // hd
    masks = [(lane == h).astype(BF) for h in range(HEADS)]
    ones = jnp.concatenate([jnp.broadcast_to(mask, (sect, ch)) for mask in masks], 0)

    def normed(r, c):
        x = x_ref[:, r, c].astype(F32).reshape(sect, ch)
        return (x * lax.rsqrt(jnp.mean(x * x, -1, keepdims=True) + 1e-6)).astype(BF)

    def scores(qkv):
        keys = jnp.concatenate([qkv[:, ch : 2 * ch] * mask for mask in masks], 0)
        return lax.dot_general(qkv[:, :ch], keys, (((1,), (1,)), ((), ())), preferred_element_type=F32)

    def weights(s):
        out = []
        for h in range(HEADS):
            part = s[:, h * sect : (h + 1) * sect]
            out.append(jnp.exp2((part - jnp.max(part, -1, keepdims=True)) * scale).astype(BF))
        return jnp.concatenate(out, 1)

    def mix(qkv, p):
        values = jnp.concatenate([qkv[:, 2 * ch :] * mask for mask in masks], 0)
        return jnp.dot(p, jnp.concatenate([values, ones], 1), preferred_element_type=F32)

    cells = [(r, c) for r in range(rows) for c in range(cols)]
    for g in range(0, len(cells), GROUP):
        some = cells[g : g + GROUP]
        n = jnp.concatenate([normed(r, c) for r, c in some], 0)
        joint = jnp.dot(n, wq_ref[...], preferred_element_type=F32).astype(BF)
        qkvs = [joint[i * sect : (i + 1) * sect] for i in range(len(some))]
        ps = [weights(s) for s in [scores(qkv) for qkv in qkvs]]
        pvs = [mix(qkv, p) for qkv, p in zip(qkvs, ps)]
        ctx = jnp.concatenate([(pv[:, :ch] / pv[:, ch:]).astype(BF) for pv in pvs], 0)
        o = jnp.dot(ctx, wo_ref[...], preferred_element_type=F32)
        for i, (r, c) in enumerate(some):
            out_ref[:, r, c] = o[i * sect : (i + 1) * sect].reshape(parts, depth, ch).astype(BF)


def attend_block(x, w_qkv, w_out):
    cells = x.shape[1] * x.shape[2]
    return pl.pallas_call(
        attend_kernel,
        out_shape=jax.ShapeDtypeStruct(x.shape, BF),
        in_specs=[vmem()] * 3,
        out_specs=vmem(),
        cost_estimate=cost(cells * 128 * 256 * 256 * 2 * 7, 1 << 20),
        compiler_params=params(),
        name="attend_block",
    )(x, w_qkv, w_out)


def finish_kernel(mixed, returned, out_ref):
    _, _, per, depth, ch = mixed.shape
    r, half = pl.program_id(0), pl.program_id(1)
    block = out_ref.shape[1]
    n = block // per
    total = mixed[pl.ds(half * n, n), r].astype(F32) + returned[pl.ds(half * n, n), r].astype(F32)
    out_ref[0] = total.astype(BF).reshape(block, depth, ch)


def finish(mixed, returned, shape, splits=2):
    rows, cols, depth, ch = shape
    return pl.pallas_call(
        finish_kernel,
        out_shape=jax.ShapeDtypeStruct(shape, BF),
        grid=(rows, splits),
        in_specs=[vmem()] * 2,
        out_specs=pl.BlockSpec((1, cols // splits, depth, ch), lambda r, s: (r, s, 0, 0)),
        cost_estimate=cost(10**6, 2 << 20),
        compiler_params=params(),
        name="finish",
    )(mixed, returned)


def swap_rows(block, pairs):
    return lax.ppermute(block, "xy", pairs)


def block(volume, conv_first, conv_second, w_qkv, w_out):
    count, groups = lax.axis_size("xy"), lax.axis_size("gz")
    links = [(i, i + 1) for i in range(1, count - 1, 2)]
    first = [pair for i, j in links[1::2] for pair in ((i, j), (j, i))]
    second = [pair for i, j in links[0::2] for pair in ((i, j), (j, i))]
    far = swap_rows(volume, first)
    near = swap_rows(volume, [(i, i ^ 1) for i in range(count)])
    *prepared, again = prepare(volume, conv_first, conv_second)
    fars = (far, swap_rows(again, second))
    mixed = conv_block(groups, prepared, near, volume, fars)
    arrived = lax.all_to_all(mixed, "gz", 0, 0, tiled=True)
    attended = attend_block(arrived, w_qkv, w_out)
    returned = lax.all_to_all(attended, "gz", 0, 0, tiled=True)
    return finish(mixed, returned, volume.shape)


def solution(mesh):
    placed = (P("xy", None, "gz", None), P(), P(), P(), P())
    return jax.shard_map(block, mesh=mesh, in_specs=placed, out_specs=P("xy", None, "gz", None), check_vma=False)
```

time: 90 us -> 76.6 us (0.85)
  the two profiles are of different devices: /device:TPU:194 before, /device:TPU:322 now
where the time goes in v2:
time: 76.6 us; the launch traced here: 76.3 us
  blocking collectives  50 us (65%)
  waiting for transfers between devices  11.6 us (15%)
  Pallas kernels  7.18 us (9%)
  starting transfers between devices  4.54 us (6%)
  local copies, waits for them, and re-layouts  2.97 us (4%)
    all_to_all x1, blocking collectives, block(): arrived = lax.all_to_all(mixed, 'gz', 0, 0, tiled=True)  26.4 us
    all_to_all x1, blocking collectives, block(): returned = lax.all_to_all(attended, 'gz', 0, 0, tiled=True)  23.5 us
    ppermute x3, waiting for transfers between devices, swap_rows(): return lax.ppermute(block, 'xy', pairs)  11.6 us
    ppermute x3, starting transfers between devices, swap_rows(): return lax.ppermute(block, 'xy', pairs)  4.54 us
    unnamed x10, local copies, waits for them, and re-layouts  2.97 us
    pallas_call x1, Pallas kernels, attend_block(): pl.pallas_call(attend_kernel, out_shape=jax.ShapeDtypeStruct(x.shape, BF)...  2.38 us
    pallas_call x1, Pallas kernels, conv_block(): pl.pallas_call(functools.partial(conv_kernel, tile), out_shape=jax.ShapeD...  2.2 us
  transfers between devices with their start and end apart: 3, of which 1 were waited for; matrix products, arithmetic and copies ran while one was open for 0% of the time, Pallas kernels for 0%

profile of v2, /device:TPU:322, one launch (start us, length us, event | category | flops | bytes accessed | tf_op | source)
XLA Modules:
  0.0 76.3 jit_solution(4463512644153903151)
XLA Ops:
  0.0 0.0 copy-start
  0.0 1.0 %copy-done = bf16[2,128,8,128]{3,2,1,0:T(8,128)(2,1)S(1)} copy-done((bf16[2,128,8,128]{3,2,1,0:T(8,128)(2,1)S(1)}, bf16[2,128,8,128]{3,2,1,0:T(8,128)(2,1)}, u32[]{:S(2)}) %copy-start) | copy-done | bytes 524312
  1.0 0.0 copy-start.1
  1.0 1.0 %copy-done.1 = bf16[3,3,128,128]{3,2,1,0:T(8,128)(2,1)S(1)} copy-done((bf16[3,3,128,128]{3,2,1,0:T(8,128)(2,1)S(1)}, bf16[3,3,128,128]{3,2,1,0:T(8,128)(2,1)}, u32[]{:S(2)}) %copy-start.1) | copy-done | bytes 294936
  2.0 0.0 copy-start.2
  2.0 1.0 %copy-done.2 = bf16[3,3,128,128]{3,2,1,0:T(8,128)(2,1)S(1)} copy-done((bf16[3,3,128,128]{3,2,1,0:T(8,128)(2,1)S(1)}, bf16[3,3,128,128]{3,2,1,0:T(8,128)(2,1)}, u32[]{:S(2)}) %copy-start.2) | copy-done | bytes 294936
  3.0 1.2 %prepare.1 = (bf16[1536,256]{1,0:T(8,128)(2,1)S(1)}, bf16[1536,256]{1,0:T(8,128)(2,1)S(1)}, f32[2,1024,256]{2,1,0:T(8,128)S(1)}, bf16[2,128,8,128]{3,2,1,0:T(8,128)(2,1)S(1)}) custom-call(bf16[2,128,8,128]{3,2,1,0:T(8,128)(2,1)S(1)} %copy-done, bf16[3,3,128,128]{3,2,1,0:T(8,128)(2,1)S(1)} %copy-done.1, bf16[3,3,128,128]{3,2,1,0:T(8,128)(2,1)S(1)} %copy-done.2), custom_call_target="tpu_custom_call" | custom-call | flops 805306368 | bytes 4194304 | tf_op jit(solution)/shard_map/prepare/pallas_call | solution.py:69
  4.2 1.9 %collective-permute-start.2 = (bf16[2,128,8,128]{3,2,1,0:T(8,128)(2,1)S(1)}, bf16[2,128,8,128]{3,2,1,0:T(8,128)(2,1)S(1)}, u32[]{:S(2)}, u32[]{:S(2)}) collective-permute-start(bf16[2,128,8,128]{3,2,1,0:T(8,128)(2,1)S(1)} %get-tuple-element.9), channel_id=1, source_target_pairs={{16,32},{32,16},{80,96},{96,80},{144,160},{160,144},{208,224},{224... | collective-permute-start | bytes 1572872 | tf_op jit(solution)/shard_map/ppermute | solution.py:226
  6.1 1.9 %collective-permute-start = (bf16[2,128,8,128]{3,2,1,0:T(8,128)(2,1)S(1)}, bf16[2,128,8,128]{3,2,1,0:T(8,128)(2,1)S(1)}, u32[]{:S(2)}, u32[]{:S(2)}) collective-permute-start(bf16[2,128,8,128]{3,2,1,0:T(8,128)(2,1)S(1)} %copy-done), channel_id=1, source_target_pairs={{0,16},{16,0},{32,48},{48,32},{64,80},{80,64},{96,112},{112,96},{1... | collective-permute-start | bytes 1572872 | tf_op jit(solution)/shard_map/ppermute | solution.py:226
  8.0 0.7 collective-permute-start.1
  8.7 11.6 %collective-permute-done.2.far_b = bf16[2,128,8,128]{3,2,1,0:T(8,128)(2,1)S(1)} collective-permute-done((bf16[2,128,8,128]{3,2,1,0:T(8,128)(2,1)S(1)}, bf16[2,128,8,128]{3,2,1,0:T(8,128)(2,1)S(1)}, u32[]{:S(2)}, u32[]{:S(2)}) %collective-permute-start.2) | collective-permute-done | bytes 524320 | tf_op jit(solution)/shard_map/ppermute | solution.py:226
  20.3 0.0 collective-permute-done.near
  20.3 0.0 collective-permute-done.1.far_a
  20.3 0.0 copy-start.3
  20.3 0.0 copy-start.4
  20.3 2.2 %conv_block.1.mixed = bf16[16,2,8,8,128]{4,3,2,1,0:T(8,128)(2,1)S(1)} custom-call(bf16[2,128,8,128]{3,2,1,0:T(8,128)(2,1)S(1)} %collective-permute-done.near, bf16[2,128,8,128]{3,2,1,0:T(8,128)(2,1)S(1)} %copy-done, bf16[2,128,8,128]{3,2,1,0:T(8,128)(2,1)S(1)} %collective-permute-done.1.far_a, bf16[2,128,8,128]{3,2,1,0:T(8,128)(2,1)S(1)} %collective-permute-done.2.far_b, ...), custom_call_target="tpu_custom_call" | custom-call | flops 1610612736 | bytes 4194304 | tf_op jit(solution)/shard_map/conv_block/pallas_call | solution.py:130
  22.5 26.4 %all_to_all.10.x_ref = bf16[16,2,8,8,128]{4,3,2,1,0:T(8,128)(2,1)S(1)} all-to-all(bf16[16,2,8,8,128]{4,3,2,1,0:T(8,128)(2,1)S(1)} %conv_block.1.mixed), channel_id=1, replica_groups=mesh['xy'=32,'gz'=16] {'gz'}, dimensions={0} | all-to-all | bytes 1048576 | tf_op jit(solution)/shard_map/all_to_all | solution.py:239
  48.9 0.0 copy-done.3
  48.9 0.0 copy-done.4
  48.9 2.4 %attend_block.1 = bf16[16,2,8,8,128]{4,3,2,1,0:T(8,128)(2,1)S(1)} custom-call(bf16[16,2,8,8,128]{4,3,2,1,0:T(8,128)(2,1)S(1)} %all_to_all.10.x_ref, bf16[128,384]{1,0:T(8,128)(2,1)S(1)} %copy-done.3, bf16[128,128]{1,0:T(8,128)(2,1)S(1)} %copy-done.4), custom_call_target="tpu_custom_call" | custom-call | flops 1879048192 | bytes 1048576 | tf_op jit(solution)/shard_map/attend_block/pallas_call | solution.py:191
  51.3 23.5 %all_to_all.11.returned = bf16[16,2,8,8,128]{4,3,2,1,0:T(8,128)(2,1)S(1)} all-to-all(bf16[16,2,8,8,128]{4,3,2,1,0:T(8,128)(2,1)S(1)} %attend_block.1), channel_id=1, replica_groups=mesh['xy'=32,'gz'=16] {'gz'}, dimensions={0} | all-to-all | bytes 1048576 | tf_op jit(solution)/shard_map/all_to_all | solution.py:241
  74.9 1.4 %finish.1 = bf16[2,128,8,128]{3,2,1,0:T(8,128)(2,1)} custom-call(bf16[16,2,8,8,128]{4,3,2,1,0:T(8,128)(2,1)S(1)} %conv_block.1.mixed, bf16[16,2,8,8,128]{4,3,2,1,0:T(8,128)(2,1)S(1)} %all_to_all.11.returned), custom_call_target="tpu_custom_call" | custom-call | flops 1000000 | bytes 2097152 | tf_op jit(solution)/shard_map/finish/pallas_call | solution.py:213
Async XLA Ops:
  0.0 1.0 %copy-start = (bf16[2,128,8,128]{3,2,1,0:T(8,128)(2,1)S(1)}, bf16[2,128,8,128]{3,2,1,0:T(8,128)(2,1)}, u32[]{:S(2)}) copy-start(bf16[2,128,8,128]{3,2,1,0:T(8,128)(2,1)} %mid.1) | copy-start | bytes 1572868
  1.0 1.0 %copy-start.1 = (bf16[3,3,128,128]{3,2,1,0:T(8,128)(2,1)S(1)}, bf16[3,3,128,128]{3,2,1,0:T(8,128)(2,1)}, u32[]{:S(2)}) copy-start(bf16[3,3,128,128]{3,2,1,0:T(8,128)(2,1)} %raw1.1) | copy-start | bytes 884740
  2.0 1.0 %copy-start.2 = (bf16[3,3,128,128]{3,2,1,0:T(8,128)(2,1)S(1)}, bf16[3,3,128,128]{3,2,1,0:T(8,128)(2,1)}, u32[]{:S(2)}) copy-start(bf16[3,3,128,128]{3,2,1,0:T(8,128)(2,1)} %raw2.1) | copy-start | bytes 884740
  4.2 16.1 %collective-permute-start.2 = (bf16[2,128,8,128]{3,2,1,0:T(8,128)(2,1)S(1)}, bf16[2,128,8,128]{3,2,1,0:T(8,128)(2,1)S(1)}, u32[]{:S(2)}, u32[]{:S(2)}) collective-permute-start(bf16[2,128,8,128]{3,2,1,0:T(8,128)(2,1)S(1)} %get-tuple-element.9), channel_id=1, source_target_pairs={{16,32},{32,16},{80,96},{96,80},{144,160},{160,144},{208,224},{224... | collective-permute-start | bytes 1572872 | tf_op jit(solution)/shard_map/ppermute | solution.py:226
  6.1 14.2 %collective-permute-start = (bf16[2,128,8,128]{3,2,1,0:T(8,128)(2,1)S(1)}, bf16[2,128,8,128]{3,2,1,0:T(8,128)(2,1)S(1)}, u32[]{:S(2)}, u32[]{:S(2)}) collective-permute-start(bf16[2,128,8,128]{3,2,1,0:T(8,128)(2,1)S(1)} %copy-done), channel_id=1, source_target_pairs={{0,16},{16,0},{32,48},{48,32},{64,80},{80,64},{96,112},{112,96},{1... | collective-permute-start | bytes 1572872 | tf_op jit(solution)/shard_map/ppermute | solution.py:226
  8.0 12.3 %collective-permute-start.1 = (bf16[2,128,8,128]{3,2,1,0:T(8,128)(2,1)S(1)}, bf16[2,128,8,128]{3,2,1,0:T(8,128)(2,1)S(1)}, u32[]{:S(2)}, u32[]{:S(2)}) collective-permute-start(bf16[2,128,8,128]{3,2,1,0:T(8,128)(2,1)S(1)} %copy-done), channel_id=1, source_target_pairs={{48,64},{64,48},{112,128},{128,112},{176,192},{192,176},{240,256},... | collective-permute-start | bytes 1572872 | tf_op jit(solution)/shard_map/ppermute | solution.py:226
  20.3 28.7 %copy-start.3 = (bf16[128,384]{1,0:T(8,128)(2,1)S(1)}, bf16[128,384]{1,0:T(8,128)(2,1)}, u32[]{:S(2)}) copy-start(bf16[128,384]{1,0:T(8,128)(2,1)} %wq_ref.1) | copy-start | bytes 294916
  20.3 28.7 %copy-start.4 = (bf16[128,128]{1,0:T(8,128)(2,1)S(1)}, bf16[128,128]{1,0:T(8,128)(2,1)}, u32[]{:S(2)}) copy-start(bf16[128,128]{1,0:T(8,128)(2,1)} %wo_ref.1) | copy-start | bytes 98308
